TPU v7x, 32 devices: a whole 2x2x4 slice. The times are simulated.
32 devices in a mesh: row: 4 (over z), col: 4 (over y, core), ch: 2 (over x).
Axes of the slice: x: 2, y: 2, z: 4, core: 2. Of those that a mesh axis runs over, the one named last changes fastest.
Arguments:
- spectra: float32 [384, 128, 1024], P('ch', 'row', 'col'), may hold values from 0 to 1
- pixel_factor: float32 [64, 128, 1024], P(None, 'row', 'col'), may hold values from 0.1 to 1
- channel_factor: float32 [64, 384], P(None, 'ch'), may hold values from 0.1 to 1
- labels: int32 [128, 1024], P('row', 'col'), may hold values from 0 to 3
Outputs:
- smoothed_factor: float32 [64, 128, 1024], P(None, 'row', 'col')
- new_channel: float32 [64, 384], P(None, 'ch')
All inputs are finite; a program needn't handle non-finite values.
Results may differ from a plain program's by a relative error of at most 0.000068.
Values sent between devices are 32-bit elements; how exact they have to be, the bound alone decides.
A program may use at most 64 MiB of HBM per device.

v0:
```python
import jax
import jax.numpy as jnp
from jax import lax
from jax.sharding import PartitionSpec as P

SMOOTH = 3


epsilon = 1e-09


def padded_2(block, sides, width):
    for axis, dim in sides:
        count = lax.axis_size(axis)
        forward = [(i, i + 1) for i in range(count - 1)]
        backward = [(target, source) for source, target in forward]
        low = lax.ppermute(
            lax.slice_in_dim(block, block.shape[dim] - width, None, axis=dim), axis, forward
        )
        high = lax.ppermute(lax.slice_in_dim(block, 0, width, axis=dim), axis, backward)
        block = jnp.concatenate([low, block, high], axis=dim)
    return block


def coefficients(marked):
    center = marked[1:-1, 1:-1]
    result = []
    for neighbour in (marked[:-2, 1:-1], marked[2:, 1:-1], marked[1:-1, :-2], marked[1:-1, 2:]):
        result.append(
            jnp.where(neighbour == 0, 0.0, jnp.where(neighbour == center, 1.0, 0.25)).astype(
                jnp.float32
            )
        )
    return result


def smooth_once(padded, field, weights):
    combined = field + weights[0] * padded[:, :-2, 1:-1] + weights[1] * padded[:, 2:, 1:-1]
    combined = combined + weights[2] * padded[:, 1:-1, :-2] + weights[3] * padded[:, 1:-1, 2:]
    return combined / (1.0 + weights[0] + weights[1] + weights[2] + weights[3])


def lift_factor(own_factor, pixel_top, chan_gram):
    factor_rank = own_factor.shape[0]
    flat_own = own_factor.reshape(factor_rank, -1)
    lower = jnp.dot(
        chan_gram, flat_own, precision=lax.Precision.HIGHEST, preferred_element_type=jnp.float32
    )
    return (flat_own * pixel_top.reshape(factor_rank, -1) / (lower + epsilon)).reshape(
        own_factor.shape
    )


def shards(spectra, pixel_factor, channel_factor, labels):
    precise = lax.Precision.HIGHEST
    contraction = (((1,), (1,)), ((), ()))
    factor_rank, row_count, col_count = pixel_factor.shape
    flat_pixel = pixel_factor.reshape(factor_rank, row_count * col_count)
    flat_data = spectra.reshape(spectra.shape[0], row_count * col_count)
    chan_top = lax.dot_general(
        flat_pixel, flat_data, contraction, precision=precise, preferred_element_type=jnp.float32
    )
    pixel_gram = lax.dot_general(
        flat_pixel, flat_pixel, contraction, precision=precise, preferred_element_type=jnp.float32
    )
    chan_top, pixel_gram = lax.psum((chan_top, pixel_gram), ("row", "col"))
    new_channel = (
        channel_factor
        * chan_top
        / (
            jnp.dot(
                pixel_gram, channel_factor, precision=precise, preferred_element_type=jnp.float32
            )
            + epsilon
        )
    )
    part_top = jnp.dot(
        new_channel, flat_data, precision=precise, preferred_element_type=jnp.float32
    ).reshape(factor_rank, row_count, col_count)
    part_gram = lax.dot_general(
        new_channel, new_channel, contraction, precision=precise, preferred_element_type=jnp.float32
    )
    marked = labels + 1
    share_rows = row_count // lax.axis_size("ch")
    share_start = lax.axis_index("ch") * share_rows
    pixel_top = lax.psum_scatter(part_top, "ch", scatter_dimension=1, tiled=True)
    chan_gram = lax.psum(part_gram, "ch")
    own_factor = lax.dynamic_slice_in_dim(pixel_factor, share_start, share_rows, 1)
    own_marks = lax.dynamic_slice_in_dim(marked, share_start, share_rows, 0)
    field = lift_factor(own_factor, pixel_top, chan_gram)
    border_marks = padded_2(own_marks, ((("row", "ch"), 0), ("col", 1)), 1)
    weights = coefficients(border_marks)
    for iteration in range(SMOOTH):
        padded = padded_2(field, ((("row", "ch"), 1), ("col", 2)), 1)
        field = smooth_once(padded, field, weights)
    smoothed_factor = lax.all_gather(field, "ch", axis=1, tiled=True)
    return (smoothed_factor, new_channel)


def solution(mesh):
    placed = (P("ch", "row", "col"), P(None, "row", "col"), P(None, "ch"), P("row", "col"))
    return jax.shard_map(
        shards,
        mesh=mesh,
        in_specs=placed,
        out_specs=(P(None, "row", "col"), P(None, "ch")),
        check_vma=False,
    )
```

profile of v0, /device:TPU:1, one launch (start us, length us, event | category | flops | bytes accessed | tf_op | source)
XLA Modules:
  0.0 289.8 jit_solution(9528814193666715446)
XLA Ops:
  7.2 7.0 %fusion.42 = f32[64,64]{1,0:T(8,128)} fusion(f32[64,32,256]{2,1,0:T(8,128)} %param.5), kind=kOutput, calls=%fused_computation.64 | convolution fusion | flops 402653184 | bytes 2113536 | tf_op jit(solution)/shard_map/dot_general | solution.py:63
  14.2 12.2 %fusion.36 = f32[64,192]{1,0:T(8,128)} fusion(f32[192,32,256]{2,1,0:T(8,128)} %param.4, f32[64,32,256]{2,1,0:T(8,128)S(1)} %copy-done.2), kind=kOutput, calls=%fused_computation.61 | convolution fusion | flops 1207959552 | bytes 8437760 | tf_op jit(solution)/shard_map/dot_general | solution.py:60
  26.7 90.1 %all-reduce.3.cloned.1.call-done = (f32[64,64]{1,0:T(8,128)}, f32[64,192]{1,0:T(8,128)}) async-done(((f32[64,64]{1,0:T(8,128)}, f32[64,192]{1,0:T(8,128)}), (f32[64,64]{1,0:T(8,128)}, f32[64,192]{1,0:T(8,128)})) %all-reduce.3.cloned.1.call-update) | async-done | bytes 65552 | tf_op jit(solution)/shard_map/psum | solution.py:66
  117.8 11.4 %fusion = f32[64,32,256]{2,0,1:T(8,128)} fusion(f32[64,192]{1,0:T(8,128)S(1)} %fusion.41, f32[24,8,32,256]{3,2,1,0:T(8,128)} %bitcast.30), kind=kOutput, calls=%fused_computation | convolution fusion | flops 1207959552 | bytes 8437760 | tf_op jit(solution)/shard_map/dot_general | solution.py:77
  131.3 4.0 %collective-permute-start = (s32[1,256]{1,0:T(1,128)S(1)}, s32[1,256]{1,0:T(1,128)S(1)}, u32[]{:S(2)}, u32[]{:S(2)}) collective-permute-start(s32[1,256]{1,0:T(1,128)S(1)} %get-tuple-element.34), channel_id=1, source_target_pairs={{0,1},{1,8},{8,9},{9,16},{16,17},{17,24},{24,25},{2,3},{3,10},{10,... | collective-permute-start | bytes 3080 | tf_op jit(solution)/shard_map/ppermute | solution.py:17
  136.2 8.8 %psum.23 = f32[64,64]{1,0:T(8,128)S(1)} all-reduce(f32[64,64]{1,0:T(8,128)S(1)} %fusion.55), channel_id=1, replica_groups=mesh['row'=4,'col'=4,'ch'=2] {'ch'}, use_global_device_ids=true, to_apply=%region_3.0 | all-reduce | flops 4096 | bytes 32768 | tf_op jit(solution)/shard_map/psum | solution.py:87
  145.1 16.6 %reduce-scatter.2.cloned.1.call-done = f32[64,16,256]{2,0,1:T(8,128)} async-done(((f32[64,32,256]{2,0,1:T(8,128)}), f32[64,16,256]{2,0,1:T(8,128)}) %reduce-scatter.2.cloned.1.call-update) | async-done | bytes 1048592 | tf_op jit(solution)/shard_map/reduce_scatter | solution.py:86
  165.9 4.0 %collective-permute-start.1 = (f32[64,1,256]{2,0,1:T(8,128)S(1)}, f32[64,1,256]{2,0,1:T(8,128)S(1)}, u32[]{:S(2)}, u32[]{:S(2)}) collective-permute-start(f32[64,1,256]{2,0,1:T(8,128)S(1)} %copy.160), channel_id=1, source_target_pairs={{0,1},{1,8},{8,9},{9,16},{16,17},{17,24},{24,25},{2,3},{3,10},{10,... | collective-permute-start | bytes 196616 | tf_op jit(solution)/shard_map/ppermute | solution.py:17
  170.0 3.3 %collective-permute-start.6 = (s32[18,1]{1,0:T(8,128)S(1)}, s32[18,1]{1,0:T(8,128)S(1)}, u32[]{:S(2)}, u32[]{:S(2)}) collective-permute-start(s32[18,1]{1,0:T(8,128)S(1)} %get-tuple-element.31), channel_id=1, source_target_pairs={{2,0},{4,2},{6,4},{3,1},{5,3},{7,5},{10,8},{12,10},{14,12},{11,9},... | collective-permute-start | bytes 224 | tf_op jit(solution)/shard_map/ppermute | solution.py:20
  173.3 3.0 %collective-permute-start.4 = (s32[18,1]{1,0:T(8,128)S(1)}, s32[18,1]{1,0:T(8,128)S(1)}, u32[]{:S(2)}, u32[]{:S(2)}) collective-permute-start(s32[18,1]{1,0:T(8,128)S(1)} %get-tuple-element.32), channel_id=1, source_target_pairs={{0,2},{2,4},{4,6},{1,3},{3,5},{5,7},{8,10},{10,12},{12,14},{9,11},... | collective-permute-start | bytes 224 | tf_op jit(solution)/shard_map/ppermute | solution.py:17
  178.1 2.4 collective-permute-start.5
  183.3 2.2 collective-permute-done.7
  185.6 9.2 %fusion.26 = f32[64,16,256]{0,1,2:T(8,128)S(1)} fusion(f32[64,18,1]{0,1,2:T(8,128)S(1)} %collective-permute-done.7, f32[64,1,256]{0,1,2:T(1,128)S(1)} %copy.139, f32[64,16,256]{0,1,2:T(8,128)} %copy-done.1, f32[64,1,256]{0,1,2:T(1,128)S(1)} %copy.133, f32[64,18,1]{0,1,2:T(8,128)S(1)} %collective-permute-done.5, f32[16,256]{0,1:T(8,128)S(1)} %copy.145, ...), kind=kLoop, calls=%fused_computation.44 | loop fusion | flops 4456448 | bytes 2319360 | tf_op jit(solution)/shard_map/div | solution.py:40
  196.4 4.0 %collective-permute-start.8 = (f32[64,1,256]{2,0,1:T(8,128)S(1)}, f32[64,1,256]{2,0,1:T(8,128)S(1)}, u32[]{:S(2)}, u32[]{:S(2)}) collective-permute-start(f32[64,1,256]{2,0,1:T(8,128)S(1)} %copy.146), channel_id=1, source_target_pairs={{0,1},{1,8},{8,9},{9,16},{16,17},{17,24},{24,25},{2,3},{3,10},{10,... | collective-permute-start | bytes 196616 | tf_op jit(solution)/shard_map/ppermute | solution.py:17
  201.9 3.1 %collective-permute-start.10 = (f32[64,18,1]{0,1,2:T(8,128)S(1)}, f32[64,18,1]{0,1,2:T(8,128)S(1)}, u32[]{:S(2)}, u32[]{:S(2)}) collective-permute-start(f32[64,18,1]{0,1,2:T(8,128)S(1)} %get-tuple-element.21), channel_id=1, source_target_pairs={{0,2},{2,4},{4,6},{1,3},{3,5},{5,7},{8,10},{10,12},{12,14},{9,11},... | collective-permute-start | bytes 13832 | tf_op jit(solution)/shard_map/ppermute | solution.py:17
  206.9 3.1 %collective-permute-done.11 = f32[64,18,1]{0,1,2:T(8,128)S(1)} collective-permute-done((f32[64,18,1]{0,1,2:T(8,128)S(1)}, f32[64,18,1]{0,1,2:T(8,128)S(1)}, u32[]{:S(2)}, u32[]{:S(2)}) %collective-permute-start.11) | collective-permute-done | bytes 4640 | tf_op jit(solution)/shard_map/ppermute | solution.py:20
  209.9 9.2 %fusion.17 = f32[64,16,256]{0,1,2:T(8,128)S(1)} fusion(f32[64,18,1]{0,1,2:T(8,128)S(1)} %collective-permute-done.11, f32[64,1,256]{0,1,2:T(1,128)S(1)} %copy.149, f32[64,16,256]{0,1,2:T(8,128)} %copy-done, f32[64,1,256]{0,1,2:T(1,128)S(1)} %copy.147, f32[64,18,1]{0,1,2:T(8,128)S(1)} %collective-permute-done.10, f32[16,256]{0,1:T(8,128)S(1)} %copy.145, ...), kind=kLoop, calls=%fused_computation.27 | loop fusion | flops 4456448 | bytes 2319360 | tf_op jit(solution)/shard_map/div | solution.py:40
  220.8 4.6 %collective-permute-start.12 = (f32[64,1,256]{2,0,1:T(8,128)S(1)}, f32[64,1,256]{2,0,1:T(8,128)S(1)}, u32[]{:S(2)}, u32[]{:S(2)}) collective-permute-start(f32[64,1,256]{2,0,1:T(8,128)S(1)} %copy.152), channel_id=1, source_target_pairs={{0,1},{1,8},{8,9},{9,16},{16,17},{17,24},{24,25},{2,3},{3,10},{10,... | collective-permute-start | bytes 196616 | tf_op jit(solution)/shard_map/ppermute | solution.py:17
  227.0 2.7 collective-permute-start.14
  231.6 3.1 %collective-permute-done.15 = f32[64,18,1]{0,1,2:T(8,128)S(1)} collective-permute-done((f32[64,18,1]{0,1,2:T(8,128)S(1)}, f32[64,18,1]{0,1,2:T(8,128)S(1)}, u32[]{:S(2)}, u32[]{:S(2)}) %collective-permute-start.15) | collective-permute-done | bytes 4640 | tf_op jit(solution)/shard_map/ppermute | solution.py:20
  234.7 5.2 %fusion.8 = f32[64,16,256]{0,1,2:T(8,128)} fusion(f32[64,18,1]{0,1,2:T(8,128)S(1)} %collective-permute-done.15, f32[64,1,256]{0,1,2:T(1,128)S(1)} %copy.155, f32[64,16,256]{0,1,2:T(8,128)S(1)} %fusion.17, f32[64,1,256]{0,1,2:T(1,128)S(1)} %copy.153, f32[64,18,1]{0,1,2:T(8,128)S(1)} %collective-permute-done.14, f32[16,256]{0,1:T(8,128)S(1)} %copy.145, ...), kind=kLoop, calls=%fused_computation.10 | loop fusion | flops 4456448 | bytes 2319360 | tf_op jit(solution)/shard_map/div | solution.py:40
  239.9 3.5 %copy.158 = f32[64,16,256]{2,0,1:T(8,128)} copy(f32[64,16,256]{0,1,2:T(8,128)} %fusion.8) | data formatting | bytes 2097152 | tf_op jit(solution)/shard_map/div | solution.py:40
  243.4 35.8 %all-gather.2.cloned.1.call-done = f32[64,32,256]{2,0,1:T(8,128)} async-done(((f32[64,16,256]{2,0,1:T(8,128)}), f32[64,32,256]{2,0,1:T(8,128)}) %all-gather.2.cloned.1.call-update) | async-done | bytes 2097168 | tf_op jit(solution)/shard_map/all_gather | solution.py:96
  279.1 4.1 %copy.159 = f32[64,32,256]{2,1,0:T(8,128)} copy(f32[64,32,256]{2,0,1:T(8,128)} %all-gather.2.cloned.1.call-done) | data formatting | bytes 4194304
  (74 shorter events, 23.1 us)
Async XLA Ops:
  7.2 7.1 %copy-start.2 = (f32[64,32,256]{2,1,0:T(8,128)S(1)}, f32[64,32,256]{2,1,0:T(8,128)}, u32[]{:S(2)}) copy-start(f32[64,32,256]{2,1,0:T(8,128)} %param.5) | copy-start | bytes 6291460
  7.2 109.6 %all-reduce.3.cloned.1.call-start = ((), (), s32[]{:S(2)}) async-start(), calls=%async_computation.3 | async-start | bytes 196608 | tf_op jit(solution)/shard_map/psum | solution.py:66
  14.2 102.5 %copy-start.5 = (f32[64,192]{1,0:T(8,128)S(1)}, f32[64,192]{1,0:T(8,128)}, u32[]{:S(2)}) copy-start(f32[64,192]{1,0:T(8,128)} %param.6) | copy-start | bytes 147460
  26.5 135.2 %reduce-scatter.2.cloned.1.call-start = ((), (), s32[]{:S(2)}) async-start(), calls=%async_computation.1 | async-start | bytes 3145728 | tf_op jit(solution)/shard_map/reduce_scatter | solution.py:86
  117.8 18.2 %copy-start.3 = (f32[64,192]{1,0:T(8,128)}, f32[64,192]{1,0:T(8,128)S(1)}, u32[]{:S(2)}) copy-start(f32[64,192]{1,0:T(8,128)S(1)} %fusion.41) | copy-start | bytes 147460
  129.2 149.9 %all-gather.2.cloned.1.call-start = ((), (), s32[]{:S(2)}) async-start(), calls=%async_computation.2 | async-start | bytes 3145728 | tf_op jit(solution)/shard_map/all_gather | solution.py:96
  130.0 6.0 %collective-permute-start.2 = (s32[1,256]{1,0:T(1,128)S(1)}, s32[1,256]{1,0:T(1,128)S(1)}, u32[]{:S(2)}, u32[]{:S(2)}) collective-permute-start(s32[1,256]{1,0:T(1,128)S(1)} %get-tuple-element.33), channel_id=1, source_target_pairs={{1,0},{8,1},{9,8},{16,9},{17,16},{24,17},{25,24},{3,2},{10,3},{11,... | collective-permute-start | bytes 3080 | tf_op jit(solution)/shard_map/ppermute | solution.py:20
  131.3 4.7 %collective-permute-start = (s32[1,256]{1,0:T(1,128)S(1)}, s32[1,256]{1,0:T(1,128)S(1)}, u32[]{:S(2)}, u32[]{:S(2)}) collective-permute-start(s32[1,256]{1,0:T(1,128)S(1)} %get-tuple-element.34), channel_id=1, source_target_pairs={{0,1},{1,8},{8,9},{9,16},{16,17},{17,24},{24,25},{2,3},{3,10},{10,... | collective-permute-start | bytes 3080 | tf_op jit(solution)/shard_map/ppermute | solution.py:17
  164.6 13.3 %collective-permute-start.3 = (f32[64,1,256]{2,0,1:T(8,128)S(1)}, f32[64,1,256]{2,0,1:T(8,128)S(1)}, u32[]{:S(2)}, u32[]{:S(2)}) collective-permute-start(f32[64,1,256]{2,0,1:T(8,128)S(1)} %copy.161), channel_id=1, source_target_pairs={{1,0},{8,1},{9,8},{16,9},{17,16},{24,17},{25,24},{3,2},{10,3},{11,... | collective-permute-start | bytes 196616 | tf_op jit(solution)/shard_map/ppermute | solution.py:20
  165.9 12.1 %collective-permute-start.1 = (f32[64,1,256]{2,0,1:T(8,128)S(1)}, f32[64,1,256]{2,0,1:T(8,128)S(1)}, u32[]{:S(2)}, u32[]{:S(2)}) collective-permute-start(f32[64,1,256]{2,0,1:T(8,128)S(1)} %copy.160), channel_id=1, source_target_pairs={{0,1},{1,8},{8,9},{9,16},{16,17},{17,24},{24,25},{2,3},{3,10},{10,... | collective-permute-start | bytes 196616 | tf_op jit(solution)/shard_map/ppermute | solution.py:17
  170.0 12.7 %collective-permute-start.6 = (s32[18,1]{1,0:T(8,128)S(1)}, s32[18,1]{1,0:T(8,128)S(1)}, u32[]{:S(2)}, u32[]{:S(2)}) collective-permute-start(s32[18,1]{1,0:T(8,128)S(1)} %get-tuple-element.31), channel_id=1, source_target_pairs={{2,0},{4,2},{6,4},{3,1},{5,3},{7,5},{10,8},{12,10},{14,12},{11,9},... | collective-permute-start | bytes 224 | tf_op jit(solution)/shard_map/ppermute | solution.py:20
  173.3 9.4 %collective-permute-start.4 = (s32[18,1]{1,0:T(8,128)S(1)}, s32[18,1]{1,0:T(8,128)S(1)}, u32[]{:S(2)}, u32[]{:S(2)}) collective-permute-start(s32[18,1]{1,0:T(8,128)S(1)} %get-tuple-element.32), channel_id=1, source_target_pairs={{0,2},{2,4},{4,6},{1,3},{3,5},{5,7},{8,10},{10,12},{12,14},{9,11},... | collective-permute-start | bytes 224 | tf_op jit(solution)/shard_map/ppermute | solution.py:17
  177.9 5.4 %copy-start.1 = (f32[64,16,256]{0,1,2:T(8,128)}, f32[64,16,256]{0,1,2:T(8,128)S(1)}, u32[]{:S(2)}) copy-start(f32[64,16,256]{0,1,2:T(8,128)S(1)} %copy.135) | copy-start | bytes 3145732
  178.1 5.2 %collective-permute-start.5 = (f32[64,18,1]{0,1,2:T(8,128)S(1)}, f32[64,18,1]{0,1,2:T(8,128)S(1)}, u32[]{:S(2)}, u32[]{:S(2)}) collective-permute-start(f32[64,18,1]{0,1,2:T(8,128)S(1)} %get-tuple-element.23), channel_id=1, source_target_pairs={{0,2},{2,4},{4,6},{1,3},{3,5},{5,7},{8,10},{10,12},{12,14},{9,11},... | collective-permute-start | bytes 13832 | tf_op jit(solution)/shard_map/ppermute | solution.py:17
  180.5 5.0 %collective-permute-start.7 = (f32[64,18,1]{0,1,2:T(8,128)S(1)}, f32[64,18,1]{0,1,2:T(8,128)S(1)}, u32[]{:S(2)}, u32[]{:S(2)}) collective-permute-start(f32[64,18,1]{0,1,2:T(8,128)S(1)} %get-tuple-element.24), channel_id=1, source_target_pairs={{2,0},{4,2},{6,4},{3,1},{5,3},{7,5},{10,8},{12,10},{14,12},{11,9},... | collective-permute-start | bytes 13832 | tf_op jit(solution)/shard_map/ppermute | solution.py:20
  194.8 12.1 %copy-start = (f32[64,16,256]{0,1,2:T(8,128)}, f32[64,16,256]{0,1,2:T(8,128)S(1)}, u32[]{:S(2)}) copy-start(f32[64,16,256]{0,1,2:T(8,128)S(1)} %fusion.26) | copy-start | bytes 3145732
  195.0 5.4 %collective-permute-start.9 = (f32[64,1,256]{2,0,1:T(8,128)S(1)}, f32[64,1,256]{2,0,1:T(8,128)S(1)}, u32[]{:S(2)}, u32[]{:S(2)}) collective-permute-start(f32[64,1,256]{2,0,1:T(8,128)S(1)} %copy.148), channel_id=1, source_target_pairs={{1,0},{8,1},{9,8},{16,9},{17,16},{24,17},{25,24},{3,2},{10,3},{11,... | collective-permute-start | bytes 196616 | tf_op jit(solution)/shard_map/ppermute | solution.py:20
  196.4 5.3 %collective-permute-start.8 = (f32[64,1,256]{2,0,1:T(8,128)S(1)}, f32[64,1,256]{2,0,1:T(8,128)S(1)}, u32[]{:S(2)}, u32[]{:S(2)}) collective-permute-start(f32[64,1,256]{2,0,1:T(8,128)S(1)} %copy.146), channel_id=1, source_target_pairs={{0,1},{1,8},{8,9},{9,16},{16,17},{17,24},{24,25},{2,3},{3,10},{10,... | collective-permute-start | bytes 196616 | tf_op jit(solution)/shard_map/ppermute | solution.py:17
  201.9 5.0 %collective-permute-start.10 = (f32[64,18,1]{0,1,2:T(8,128)S(1)}, f32[64,18,1]{0,1,2:T(8,128)S(1)}, u32[]{:S(2)}, u32[]{:S(2)}) collective-permute-start(f32[64,18,1]{0,1,2:T(8,128)S(1)} %get-tuple-element.21), channel_id=1, source_target_pairs={{0,2},{2,4},{4,6},{1,3},{3,5},{5,7},{8,10},{10,12},{12,14},{9,11},... | collective-permute-start | bytes 13832 | tf_op jit(solution)/shard_map/ppermute | solution.py:17
  204.9 5.0 %collective-permute-start.11 = (f32[64,18,1]{0,1,2:T(8,128)S(1)}, f32[64,18,1]{0,1,2:T(8,128)S(1)}, u32[]{:S(2)}, u32[]{:S(2)}) collective-permute-start(f32[64,18,1]{0,1,2:T(8,128)S(1)} %get-tuple-element.22), channel_id=1, source_target_pairs={{2,0},{4,2},{6,4},{3,1},{5,3},{7,5},{10,8},{12,10},{14,12},{11,9},... | collective-permute-start | bytes 13832 | tf_op jit(solution)/shard_map/ppermute | solution.py:20
  219.4 6.0 %collective-permute-start.13 = (f32[64,1,256]{2,0,1:T(8,128)S(1)}, f32[64,1,256]{2,0,1:T(8,128)S(1)}, u32[]{:S(2)}, u32[]{:S(2)}) collective-permute-start(f32[64,1,256]{2,0,1:T(8,128)S(1)} %copy.154), channel_id=1, source_target_pairs={{1,0},{8,1},{9,8},{16,9},{17,16},{24,17},{25,24},{3,2},{10,3},{11,... | collective-permute-start | bytes 196616 | tf_op jit(solution)/shard_map/ppermute | solution.py:20
  220.8 6.0 %collective-permute-start.12 = (f32[64,1,256]{2,0,1:T(8,128)S(1)}, f32[64,1,256]{2,0,1:T(8,128)S(1)}, u32[]{:S(2)}, u32[]{:S(2)}) collective-permute-start(f32[64,1,256]{2,0,1:T(8,128)S(1)} %copy.152), channel_id=1, source_target_pairs={{0,1},{1,8},{8,9},{9,16},{16,17},{17,24},{24,25},{2,3},{3,10},{10,... | collective-permute-start | bytes 196616 | tf_op jit(solution)/shard_map/ppermute | solution.py:17
  227.0 4.6 %collective-permute-start.14 = (f32[64,18,1]{0,1,2:T(8,128)S(1)}, f32[64,18,1]{0,1,2:T(8,128)S(1)}, u32[]{:S(2)}, u32[]{:S(2)}) collective-permute-start(f32[64,18,1]{0,1,2:T(8,128)S(1)} %get-tuple-element.19), channel_id=1, source_target_pairs={{0,2},{2,4},{4,6},{1,3},{3,5},{5,7},{8,10},{10,12},{12,14},{9,11},... | collective-permute-start | bytes 13832 | tf_op jit(solution)/shard_map/ppermute | solution.py:17
  229.7 5.0 %collective-permute-start.15 = (f32[64,18,1]{0,1,2:T(8,128)S(1)}, f32[64,18,1]{0,1,2:T(8,128)S(1)}, u32[]{:S(2)}, u32[]{:S(2)}) collective-permute-start(f32[64,18,1]{0,1,2:T(8,128)S(1)} %get-tuple-element.20), channel_id=1, source_target_pairs={{2,0},{4,2},{6,4},{3,1},{5,3},{7,5},{10,8},{12,10},{14,12},{11,9},... | collective-permute-start | bytes 13832 | tf_op jit(solution)/shard_map/ppermute | solution.py:20
  (1 other events, 0.8 us)
Sparse Core Ops, SparseCore 0:
  26.6 90.1 all-reduce.2
  129.3 32.2 reduce-scatter.1
  243.5 35.5 all-gather.1
where the time goes:
time: 292 us; the launch traced here: 290 us
  waiting for transfers between devices  153 us (52%)
  starting transfers between devices  42.5 us (15%)
  matrix products  33 us (11%)
  other arithmetic  23.7 us (8%)
  between operations  14.2 us (5%)
  local copies, waits for them, and re-layouts  14.1 us (5%)
  blocking collectives  8.84 us (3%)
    psum x1, waiting for transfers between devices, shards(): chan_top, pixel_gram = lax.psum((chan_top, pixel_gram), ('row', 'col'))  90.1 us
    all_gather x1, waiting for transfers between devices, shards(): smoothed_factor = lax.all_gather(field, 'ch', axis=1, tiled=True)  35.8 us
    ppermute x8, starting transfers between devices, padded_2(): lax.ppermute(lax.slice_in_dim(block, block.shape[dim] - width, None, axis...  27.8 us
    div x3, other arithmetic, smooth_once(): return combined / (1.0 + weights[0] + weights[1] + weights[2] + weights[3])  23.6 us
    reduce_scatter x1, waiting for transfers between devices, shards(): lax.psum_scatter(part_top, 'ch', scatter_dimension=1, tiled=True)  16.6 us
    ppermute x8, starting transfers between devices, padded_2(): lax.ppermute(lax.slice_in_dim(block, 0, width, axis=dim), axis, backward)  14.5 us
    dot_general x1, matrix products, shards(): lax.dot_general(flat_pixel, flat_data, contraction, precision=precise, pr...  12.2 us
    dot_general x1, matrix products, shards(): jnp.dot(new_channel, flat_data, precision=precise, preferred_element_type...  11.4 us
  transfers between devices with their start and end apart: 19, of which 8 were waited for; matrix products, arithmetic and copies ran while one was open for 1% of the time, Pallas kernels for 0%

commit v1 on v0

v1 whole, which is shorter than its diff:
```python
import functools

import jax
import jax.numpy as jnp
from jax import lax
from jax.experimental import pallas as pl
from jax.experimental.pallas import tpu as pltpu
from jax.sharding import PartitionSpec as P

SMOOTH = 3
MESH = pl.DeviceIdType.MESH
LANES = 128
SUB = 8
CHUNK = 4

epsilon = 1e-09


def split(value):
    high = value.astype(jnp.bfloat16)
    low = (value - high.astype(jnp.float32)).astype(jnp.bfloat16)
    return high, low


def dot(left, right, contraction):
    return lax.dot_general(
        left, right, (contraction, ((), ())), preferred_element_type=jnp.float32
    )


def dot3(left, right, contraction):
    rows = left[0].shape[0]
    both = dot(jnp.concatenate(left, axis=0), right[0], contraction)
    return both[:rows] + both[rows:] + dot(left[0], right[1], contraction)


NT = ((1,), (1,))
NN = ((1,), (0,))


def factor_kernel(
    sizes, x_hbm, w_hbm, cf_ref, lab_ref, field_out, nc_out,
    xw, gram, gram_in, gram_row, nc, part, field, left, right,
    load_sem, g_send, g_recv, z_send, z_recv, n_send, n_recv,
    t_send, t_recv, c_send, c_recv, r_send, r_recv, out_sem,
):
    n_row, n_col, n_ch = sizes
    rank, rows, cols = w_hbm.shape
    chans = x_hbm.shape[0]
    share = rank // n_col
    chunks = rows // CHUNK
    me_row, me_col, me_ch = (lax.axis_index(a) for a in ("row", "col", "ch"))

    def load(r):
        return (
            pltpu.make_async_copy(w_hbm.at[:, r, :], xw.at[r, pl.ds(0, rank), :], load_sem.at[0, r]),
            pltpu.make_async_copy(x_hbm.at[:, r, :], xw.at[r, pl.ds(rank, chans), :], load_sem.at[1, r]),
        )

    for r in range(rows):
        for copy in load(r):
            copy.start()

    barrier = pltpu.get_barrier_semaphore()
    for d in range(1, n_row):
        pl.semaphore_signal(
            barrier, inc=1, device_id={"row": lax.rem(me_row + d, n_row)}, device_id_type=MESH
        )
    for d in range(1, n_col * n_ch):
        pl.semaphore_signal(
            barrier, inc=1, device_id=side(me_col, me_ch, d, n_col, n_ch), device_id_type=MESH
        )

    for buffer in (left, right):
        edge = 0 if buffer is left else n_col - 1

        @pl.when(me_col == edge)
        def _():
            buffer[...] = jnp.zeros_like(buffer)

    for at, edge in ((0, 0), (rows + SMOOTH, n_row - 1)):

        @pl.when(me_row == edge)
        def _():
            field[pl.ds(at, SMOOTH)] = jnp.zeros((SMOOTH,) + field.shape[1:], jnp.float32)

    def marks(r, carry):
        row = (lab_ref[pl.ds(r, 1), :] + 1).astype(jnp.float32)
        field[r + SMOOTH, pl.ds(rank, SUB), pl.ds(0, cols)] = jnp.broadcast_to(row, (SUB, cols))
        return carry

    lax.fori_loop(0, rows, marks, 0)

    gram[...] = jnp.zeros_like(gram)
    for r in range(rows):
        for copy in load(r):
            copy.wait()
        high, low = split(xw[r])
        total = dot3((high[:rank], low[:rank]), (high, low), NT)
        gram[...] += total.reshape(gram.shape)

    pl.semaphore_wait(barrier, n_row - 1 + n_col * n_ch - 1)

    def to_col(d):
        peer = lax.rem(me_col + d, n_col)
        return pltpu.make_async_remote_copy(
            gram.at[peer], gram_in.at[d - 1], g_send.at[d - 1], g_recv.at[d - 1],
            device_id={"col": peer}, device_id_type=MESH,
        )

    for d in range(1, n_col):
        to_col(d).start()
    own = gram[me_col]
    for d in range(1, n_col):
        to_col(d).wait_recv()
        own = own + gram_in[d - 1]
    gram_row[me_row] = own

    def to_row(d):
        peer = lax.rem(me_row + d, n_row)
        return pltpu.make_async_remote_copy(
            gram_row.at[me_row], gram_row.at[me_row], z_send.at[d - 1], z_recv.at[d - 1],
            device_id={"row": peer}, device_id_type=MESH,
        )

    def from_row(d):
        peer = lax.rem(me_row + n_row - d, n_row)
        return pltpu.make_async_remote_copy(
            gram_row.at[peer], gram_row.at[peer], z_send.at[d - 1], z_recv.at[d - 1],
            device_id={"row": peer}, device_id_type=MESH,
        )

    for d in range(1, n_row):
        to_row(d).start()
    for d in range(1, n_row):
        from_row(d).wait_recv()
    total = gram_row[0]
    for z in range(1, n_row):
        total = total + gram_row[z]
    lower = jnp.dot(
        total[:, :rank], cf_ref[...], precision=lax.Precision.HIGHEST,
        preferred_element_type=jnp.float32,
    )
    own_cf = cf_ref[pl.ds(pl.multiple_of(me_col * share, share), share), :]
    nc[me_ch, me_col] = own_cf * total[:, rank:] / (lower + epsilon)

    def to_side(d):
        return pltpu.make_async_remote_copy(
            nc.at[me_ch, me_col], nc.at[me_ch, me_col], n_send.at[d - 1], n_recv.at[d - 1],
            device_id=side(me_col, me_ch, d, n_col, n_ch), device_id_type=MESH,
        )

    def from_side(d):
        at = side(me_col, me_ch, n_col * n_ch - d, n_col, n_ch)
        slot = nc.at[at["ch"], at["col"]]
        return pltpu.make_async_remote_copy(
            slot, slot, n_send.at[d - 1], n_recv.at[d - 1],
            device_id=at, device_id_type=MESH,
        )

    for d in range(1, n_col * n_ch):
        to_side(d).start()
    for d in range(1, n_col * n_ch):
        from_side(d).wait_recv()

    mine = nc[me_ch].reshape(rank, chans)
    nc_out[...] = mine
    mine = split(mine)

    def chunk_of(i):
        return lax.rem(i + chunks - 1, chunks)

    def to_ch(d, c):
        peer = lax.rem(me_ch + d, n_ch)
        slot = part.at[me_ch, pl.ds(c * CHUNK, CHUNK)]
        return pltpu.make_async_remote_copy(
            slot, slot, t_send.at[d - 1, c], t_recv.at[d - 1, c],
            device_id={"ch": peer}, device_id_type=MESH,
        )

    def from_ch(d, c):
        peer = lax.rem(me_ch + n_ch - d, n_ch)
        slot = part.at[peer, pl.ds(c * CHUNK, CHUNK)]
        return pltpu.make_async_remote_copy(
            slot, slot, t_send.at[d - 1, c], t_recv.at[d - 1, c],
            device_id={"ch": peer}, device_id_type=MESH,
        )

    def send_part(i, carry):
        c = chunk_of(i)
        for k in range(CHUNK):
            r = c * CHUNK + k
            part[me_ch, r] = dot3(mine, split(xw[r, pl.ds(rank, chans), :]), NN)
        for d in range(1, n_ch):
            to_ch(d, c).start()
        return carry

    lax.fori_loop(0, chunks, send_part, 0)

    cg = jnp.zeros((rank, rank), jnp.float32)
    for h in range(n_ch):
        block = nc[h].reshape(rank, chans)
        cg = cg + lax.dot_general(
            block, block, (NT, ((), ())), precision=lax.Precision.HIGHEST,
            preferred_element_type=jnp.float32,
        )
    cg = split(cg)

    def to_right(c):
        return pltpu.make_async_remote_copy(
            field.at[pl.ds(c * CHUNK + SMOOTH, CHUNK), :, pl.ds(cols - LANES, LANES)],
            left.at[pl.ds(c * CHUNK, CHUNK)], c_send.at[0, c], c_recv.at[0, c],
            device_id={"col": lax.rem(me_col + 1, n_col)}, device_id_type=MESH,
        )

    def to_left(c):
        return pltpu.make_async_remote_copy(
            field.at[pl.ds(c * CHUNK + SMOOTH, CHUNK), :, pl.ds(0, LANES)],
            right.at[pl.ds(c * CHUNK, CHUNK)], c_send.at[1, c], c_recv.at[1, c],
            device_id={"col": lax.rem(me_col + n_col - 1, n_col)}, device_id_type=MESH,
        )

    def raise_chunk(i):
        c = chunk_of(i)
        for d in range(1, n_ch):
            from_ch(d, c).wait_recv()
        for k in range(CHUNK):
            r = c * CHUNK + k
            w = xw[r, pl.ds(0, rank), :]
            top = part[0, r]
            for h in range(1, n_ch):
                top = top + part[h, r]
            low = dot3(cg, split(w), NN)
            field[r + SMOOTH, pl.ds(0, rank), pl.ds(0, cols)] = w * top / (low + epsilon)

        @pl.when(me_col < n_col - 1)
        def _():
            to_right(c).start()

        @pl.when(me_col > 0)
        def _():
            to_left(c).start()

    lane = lax.broadcasted_iota(jnp.int32, (CHUNK, rank + SUB, LANES), 2)

    def widen_chunk(i):
        c = chunk_of(i)

        @pl.when(me_col > 0)
        def _():
            to_right(c).wait_recv()

        @pl.when(me_col < n_col - 1)
        def _():
            to_left(c).wait_recv()

        from_right = jnp.where(lane < SMOOTH, right[pl.ds(c * CHUNK, CHUNK)], 0.0)
        wide = jnp.where(lane >= LANES - SMOOTH, left[pl.ds(c * CHUNK, CHUNK)], from_right)
        field[pl.ds(c * CHUNK + SMOOTH, CHUNK), :, pl.ds(cols, LANES)] = wide

    def to_down():
        return pltpu.make_async_remote_copy(
            field.at[pl.ds(rows, SMOOTH)], field.at[pl.ds(0, SMOOTH)], r_send.at[0], r_recv.at[0],
            device_id={"row": lax.rem(me_row + 1, n_row)}, device_id_type=MESH,
        )

    def to_up():
        return pltpu.make_async_remote_copy(
            field.at[pl.ds(SMOOTH, SMOOTH)], field.at[pl.ds(rows + SMOOTH, SMOOTH)],
            r_send.at[1], r_recv.at[1],
            device_id={"row": lax.rem(me_row + n_row - 1, n_row)}, device_id_type=MESH,
        )

    raise_chunk(0)
    raise_chunk(1)
    widen_chunk(0)
    raise_chunk(2)
    widen_chunk(1)

    @pl.when(me_row < n_row - 1)
    def _():
        to_down().start()

    @pl.when(me_row > 0)
    def _():
        to_up().start()

    def step(i, carry):
        raise_chunk(i)
        widen_chunk(i - 1)
        return carry

    lax.fori_loop(3, chunks, step, 0)
    widen_chunk(chunks - 1)

    @pl.when(me_row > 0)
    def _():
        to_down().wait_recv()

    @pl.when(me_row < n_row - 1)
    def _():
        to_up().wait_recv()

    out = pltpu.make_async_copy(field, field_out, out_sem)
    out.start()

    for d in range(1, n_col):
        to_col(d).wait_send()
    for d in range(1, n_row):
        to_row(d).wait_send()
    for d in range(1, n_col * n_ch):
        to_side(d).wait_send()

    def drain(c, carry):
        for d in range(1, n_ch):
            to_ch(d, c).wait_send()

        @pl.when(me_col < n_col - 1)
        def _():
            to_right(c).wait_send()

        @pl.when(me_col > 0)
        def _():
            to_left(c).wait_send()

        return carry

    lax.fori_loop(0, chunks, drain, 0)

    @pl.when(me_row < n_row - 1)
    def _():
        to_down().wait_send()

    @pl.when(me_row > 0)
    def _():
        to_up().wait_send()

    out.wait()


def side(me_col, me_ch, d, n_col, n_ch):
    place = lax.rem(me_col * n_ch + me_ch + d, n_col * n_ch)
    return {"col": place // n_ch, "ch": lax.rem(place, n_ch)}


def smooth_kernel(field_ref, out_hbm, weight, first, second, done, out_sem):
    rank, rows, cols = out_hbm.shape
    wide = field_ref.shape[2]
    groups = rank // SUB

    def coefficients(e, carry):
        center = field_ref[e, pl.ds(rank, SUB), :]
        around = (
            field_ref[e - 1, pl.ds(rank, SUB), :],
            field_ref[e + 1, pl.ds(rank, SUB), :],
            pltpu.roll(center, 1, 1),
            pltpu.roll(center, wide - 1, 1),
        )
        parts = [
            jnp.where(near == 0, 0.0, jnp.where(near == center, 1.0, 0.25)) for near in around
        ]
        scale = 1.0 / (1.0 + parts[0] + parts[1] + parts[2] + parts[3])
        weight[e, 0] = scale
        for j in range(4):
            weight[e, j + 1] = parts[j] * scale
        return carry

    lax.fori_loop(1, rows + 2 * SMOOTH - 1, coefficients, 0)

    def smooth(source, e):
        here = source[e, pl.ds(0, rank), :].reshape(groups, SUB, wide)
        up = source[e - 1, pl.ds(0, rank), :].reshape(groups, SUB, wide)
        down = source[e + 1, pl.ds(0, rank), :].reshape(groups, SUB, wide)
        total = weight[e, 0] * here + weight[e, 1] * up + weight[e, 2] * down
        total = total + weight[e, 3] * pltpu.roll(here, 1, 2)
        total = total + weight[e, 4] * pltpu.roll(here, wide - 1, 2)
        return total.reshape(rank, wide)

    def one(e, carry):
        first[e] = smooth(field_ref, e)
        return carry

    def two(e, carry):
        second[e] = smooth(first, e)
        return carry

    def put(r):
        return pltpu.make_async_copy(done.at[r], out_hbm.at[:, r, :], out_sem.at[r])

    lax.fori_loop(1, rows + 5, one, 0)
    lax.fori_loop(2, rows + 4, two, 0)
    for r in range(rows):
        done[r] = smooth(second, r + SMOOTH)[:, :cols]
        put(r).start()
    for r in range(rows):
        put(r).wait()


def shards(sizes, spectra, pixel_factor, channel_factor, labels):
    n_row, n_col, n_ch = sizes
    rank, rows, cols = pixel_factor.shape
    chans = spectra.shape[0]
    share = rank // n_col
    chunks = rows // CHUNK
    tall = rows + 2 * SMOOTH
    wide = cols + LANES
    f32 = jnp.float32
    vmem = pl.BlockSpec(memory_space=pltpu.VMEM)
    anywhere = pl.BlockSpec(memory_space=pl.ANY)
    dma = pltpu.SemaphoreType.DMA
    field, new_channel = pl.pallas_call(
        functools.partial(factor_kernel, sizes),
        out_shape=(
            jax.ShapeDtypeStruct((tall, rank + SUB, wide), f32),
            jax.ShapeDtypeStruct(channel_factor.shape, f32),
        ),
        in_specs=[anywhere, anywhere, vmem, vmem],
        out_specs=(anywhere, vmem),
        scratch_shapes=[
            pltpu.VMEM((rows, rank + chans, cols), f32),
            pltpu.VMEM((n_col, share, rank + chans), f32),
            pltpu.VMEM((n_col - 1, share, rank + chans), f32),
            pltpu.VMEM((n_row, share, rank + chans), f32),
            pltpu.VMEM((n_ch, n_col, share, chans), f32),
            pltpu.VMEM((n_ch, rows, rank, cols), f32),
            pltpu.VMEM((tall, rank + SUB, wide), f32),
            pltpu.VMEM((rows, rank + SUB, LANES), f32),
            pltpu.VMEM((rows, rank + SUB, LANES), f32),
            dma((2, rows)),
            dma((n_col - 1,)), dma((n_col - 1,)),
            dma((n_row - 1,)), dma((n_row - 1,)),
            dma((n_col * n_ch - 1,)), dma((n_col * n_ch - 1,)),
            dma((n_ch - 1, chunks)), dma((n_ch - 1, chunks)),
            dma((2, chunks)), dma((2, chunks)),
            dma((2,)), dma((2,)),
            dma,
        ],
        compiler_params=pltpu.CompilerParams(
            collective_id=0, has_side_effects=True, vmem_limit_bytes=60 * 1024 * 1024
        ),
        name="factor",
    )(spectra, pixel_factor, channel_factor, labels)
    smoothed = pl.pallas_call(
        smooth_kernel,
        out_shape=jax.ShapeDtypeStruct(pixel_factor.shape, f32),
        in_specs=[vmem],
        out_specs=anywhere,
        scratch_shapes=[
            pltpu.VMEM((tall, 5, SUB, wide), f32),
            pltpu.VMEM((tall, rank, wide), f32),
            pltpu.VMEM((tall, rank, wide), f32),
            pltpu.VMEM((rows, rank, cols), f32),
            dma((rows,)),
        ],
        compiler_params=pltpu.CompilerParams(vmem_limit_bytes=48 * 1024 * 1024),
        name="smooth",
    )(field)
    return smoothed, new_channel


def solution(mesh):
    sizes = tuple(mesh.shape[a] for a in ("row", "col", "ch"))
    placed = (P("ch", "row", "col"), P(None, "row", "col"), P(None, "ch"), P("row", "col"))
    return jax.shard_map(
        functools.partial(shards, sizes),
        mesh=mesh,
        in_specs=placed,
        out_specs=(P(None, "row", "col"), P(None, "ch")),
        check_vma=False,
    )
```

time: 292 us -> 95.9 us (0.33)
  waiting for transfers between devices: 153 us -> 0 us
  Pallas kernels: 0 us -> 92.2 us
  starting transfers between devices: 42.5 us -> 0 us
  matrix products: 33 us -> 0 us
  other arithmetic: 23.7 us -> 0 us
  between operations: 14.2 us -> 0.66 us
  local copies, waits for them, and re-layouts: 14.1 us -> 2.82 us
  blocking collectives: 8.84 us -> 0 us
    pallas_call x0 -> x2, Pallas kernels: none -> 92.2 us  [the longest x1 75.7 us: shards(): pl.pallas_call(functools.partial(factor_kernel, sizes), out_shape=(jax.Sh...]
    psum x1 -> x0, waiting for transfers between devices: 90.1 us -> none  [shards(): chan_top, pixel_gram = lax.psum((chan_top, pixel_gram), ('row', 'col'))]
    ppermute x16 -> x0, starting transfers between devices: 42.2 us -> none  [the longest x8 27.8 us: padded_2(): lax.ppermute(lax.slice_in_dim(block, block.shape[dim] - width, None, axis...]
    all_gather x1 -> x0, waiting for transfers between devices: 35.8 us -> none  [shards(): smoothed_factor = lax.all_gather(field, 'ch', axis=1, tiled=True)]
    dot_general x6 -> x0, matrix products: 33 us -> none  [the longest x1 12.2 us: shards(): lax.dot_general(flat_pixel, flat_data, contraction, precision=precise, pr...]
    div x3 -> x0, other arithmetic: 23.6 us -> none  [smooth_once(): return combined / (1.0 + weights[0] + weights[1] + weights[2] + weights[3])]
    reduce_scatter x1 -> x0, waiting for transfers between devices: 16.6 us -> none  [shards(): lax.psum_scatter(part_top, 'ch', scatter_dimension=1, tiled=True)]
    ppermute x16 -> x0, waiting for transfers between devices: 10.9 us -> none  [the longest x8 8.38 us: padded_2(): lax.ppermute(lax.slice_in_dim(block, 0, width, axis=dim), axis, backward)]
  transfers between devices with their start and end apart: 19 -> 0, of which waited for: 8 -> 0; matrix products, arithmetic and copies ran while one was open for 1% -> 0% of each run, Pallas kernels for 0% -> 0%
where the time goes in v1:
time: 95.9 us; the launch traced here: 95.7 us
  Pallas kernels  92.2 us (96%)
  local copies, waits for them, and re-layouts  2.82 us (3%)
    pallas_call x1, Pallas kernels, shards(): pl.pallas_call(functools.partial(factor_kernel, sizes), out_shape=(jax.Sh...  75.7 us
    pallas_call x1, Pallas kernels, shards(): pl.pallas_call(smooth_kernel, out_shape=jax.ShapeDtypeStruct(pixel_factor...  16.5 us
    unnamed x5, local copies, waits for them, and re-layouts  2.82 us

profile of v1, /device:TPU:1, one launch (start us, length us, event | category | flops | bytes accessed | tf_op | source)
XLA Modules:
  0.0 95.7 jit_solution(14743249774002261147)
XLA Ops:
  0.6 75.7 %factor.1 = (f32[38,72,384]{2,1,0:T(8,128)}, f32[64,192]{1,0:T(8,128)}) custom-call(f32[192,32,256]{2,1,0:T(8,128)} %x_hbm.1, f32[64,32,256]{2,1,0:T(8,128)} %w_hbm.1, f32[64,192]{1,0:T(8,128)} %cf_ref.1, s32[32,256]{1,0:T(8,128)} %lab_ref.1), custom_call_target="tpu_custom_call" | custom-call | tf_op jit(solution)/shard_map/factor/pallas_call | solution.py:411
  76.3 0.0 copy-start
  76.3 2.2 %copy-done = f32[38,72,384]{2,1,0:T(8,128)S(1)} copy-done((f32[38,72,384]{2,1,0:T(8,128)S(1)}, f32[38,72,384]{2,1,0:T(8,128)}, u32[]{:S(2)}) %copy-start) | copy-done | bytes 4202520
  78.5 0.0 copy-start.1
  78.5 16.5 %smooth.1 = f32[64,32,256]{2,1,0:T(8,128)} custom-call(f32[38,72,384]{2,1,0:T(8,128)S(1)} %copy-done), custom_call_target="tpu_custom_call" | custom-call | tf_op jit(solution)/shard_map/smooth/pallas_call | solution.py:443
  95.0 0.0 copy-done.1
  95.0 0.6 copy.7
Async XLA Ops:
  76.3 2.2 %copy-start = (f32[38,72,384]{2,1,0:T(8,128)S(1)}, f32[38,72,384]{2,1,0:T(8,128)}, u32[]{:S(2)}) copy-start(f32[38,72,384]{2,1,0:T(8,128)} %get-tuple-element.4.field_ref) | copy-start | bytes 12607492
  78.5 16.5 %copy-start.1 = (f32[64,192]{1,0:T(8,128)S(1)}, f32[64,192]{1,0:T(8,128)}, u32[]{:S(2)}) copy-start(f32[64,192]{1,0:T(8,128)} %get-tuple-element.9) | copy-start | bytes 147460

commit v2 on v1

--- a/solution.py
+++ b/solution.py
@@ -11,7 +11,9 @@
 MESH = pl.DeviceIdType.MESH
 LANES = 128
 SUB = 8
-CHUNK = 4
+CHUNK = 2
+EDGE = -(-SMOOTH // CHUNK)
+LAG = 3
 
 epsilon = 1e-09
 
@@ -39,9 +41,9 @@
 
 
 def factor_kernel(
-    sizes, x_hbm, w_hbm, cf_ref, lab_ref, field_out, nc_out,
-    xw, gram, gram_in, gram_row, nc, part, field, left, right,
-    load_sem, g_send, g_recv, z_send, z_recv, n_send, n_recv,
+    sizes, x_hbm, w_hbm, cf_ref, lab_ref, out_hbm, nc_out,
+    xw, other, gram, gram_in, gram_row, nc, part, field, left, right, weight, first, second, done,
+    load_sem, e_send, e_recv, g_send, g_recv, z_send, z_recv, n_send, n_recv,
     t_send, t_recv, c_send, c_recv, r_send, r_recv, out_sem,
 ):
     n_row, n_col, n_ch = sizes
@@ -49,6 +51,8 @@
     chans = x_hbm.shape[0]
     share = rank // n_col
     chunks = rows // CHUNK
+    early = rows - EDGE * CHUNK
+    wide = cols + LANES
     me_row, me_col, me_ch = (lax.axis_index(a) for a in ("row", "col", "ch"))
 
     def load(r):
@@ -57,7 +61,8 @@
             pltpu.make_async_copy(x_hbm.at[:, r, :], xw.at[r, pl.ds(rank, chans), :], load_sem.at[1, r]),
         )
 
-    for r in range(rows):
+    order = tuple(range(early, rows)) + tuple(range(early))
+    for r in order:
         for copy in load(r):
             copy.start()
 
@@ -92,14 +97,27 @@
     lax.fori_loop(0, rows, marks, 0)
 
     gram[...] = jnp.zeros_like(gram)
-    for r in range(rows):
+
+    def to_early(d):
+        return pltpu.make_async_remote_copy(
+            xw.at[pl.ds(early, rows - early), pl.ds(rank, chans), :], other.at[d - 1],
+            e_send.at[d - 1], e_recv.at[d - 1],
+            device_id={"ch": lax.rem(me_ch + d, n_ch)}, device_id_type=MESH,
+        )
+
+    for r in order[: rows - early]:
         for copy in load(r):
             copy.wait()
+    pl.semaphore_wait(barrier, n_row - 1 + n_col * n_ch - 1)
+    for d in range(1, n_ch):
+        to_early(d).start()
+    for i, r in enumerate(order):
+        if i >= rows - early:
+            for copy in load(r):
+                copy.wait()
         high, low = split(xw[r])
         total = dot3((high[:rank], low[:rank]), (high, low), NT)
         gram[...] += total.reshape(gram.shape)
-
-    pl.semaphore_wait(barrier, n_row - 1 + n_col * n_ch - 1)
 
     def to_col(d):
         peer = lax.rem(me_col + d, n_col)
@@ -168,7 +186,7 @@
     mine = split(mine)
 
     def chunk_of(i):
-        return lax.rem(i + chunks - 1, chunks)
+        return lax.rem(i + chunks - EDGE, chunks)
 
     def to_ch(d, c):
         peer = lax.rem(me_ch + d, n_ch)
@@ -195,7 +213,16 @@
             to_ch(d, c).start()
         return carry
 
-    lax.fori_loop(0, chunks, send_part, 0)
+    lax.fori_loop(EDGE, chunks, send_part, 0)
+
+    for r in range(early, rows):
+        part[me_ch, r] = dot3(mine, split(xw[r, pl.ds(rank, chans), :]), NN)
+    for d in range(1, n_ch):
+        peer = lax.rem(me_ch + n_ch - d, n_ch)
+        theirs = split(nc[peer].reshape(rank, chans))
+        to_early(d).wait_recv()
+        for r in range(early, rows):
+            part[peer, r] = dot3(theirs, split(other[d - 1, r - early]), NN)
 
     cg = jnp.zeros((rank, rank), jnp.float32)
     for h in range(n_ch):
@@ -220,10 +247,11 @@
             device_id={"col": lax.rem(me_col + n_col - 1, n_col)}, device_id_type=MESH,
         )
 
-    def raise_chunk(i):
+    def raise_chunk(i, awaited=True):
         c = chunk_of(i)
-        for d in range(1, n_ch):
-            from_ch(d, c).wait_recv()
+        if awaited:
+            for d in range(1, n_ch):
+                from_ch(d, c).wait_recv()
         for k in range(CHUNK):
             r = c * CHUNK + k
             w = xw[r, pl.ds(0, rank), :]
@@ -271,88 +299,11 @@
             device_id={"row": lax.rem(me_row + n_row - 1, n_row)}, device_id_type=MESH,
         )
 
-    raise_chunk(0)
-    raise_chunk(1)
-    widen_chunk(0)
-    raise_chunk(2)
-    widen_chunk(1)
-
-    @pl.when(me_row < n_row - 1)
-    def _():
-        to_down().start()
-
-    @pl.when(me_row > 0)
-    def _():
-        to_up().start()
-
-    def step(i, carry):
-        raise_chunk(i)
-        widen_chunk(i - 1)
-        return carry
-
-    lax.fori_loop(3, chunks, step, 0)
-    widen_chunk(chunks - 1)
-
-    @pl.when(me_row > 0)
-    def _():
-        to_down().wait_recv()
-
-    @pl.when(me_row < n_row - 1)
-    def _():
-        to_up().wait_recv()
-
-    out = pltpu.make_async_copy(field, field_out, out_sem)
-    out.start()
-
-    for d in range(1, n_col):
-        to_col(d).wait_send()
-    for d in range(1, n_row):
-        to_row(d).wait_send()
-    for d in range(1, n_col * n_ch):
-        to_side(d).wait_send()
-
-    def drain(c, carry):
-        for d in range(1, n_ch):
-            to_ch(d, c).wait_send()
-
-        @pl.when(me_col < n_col - 1)
-        def _():
-            to_right(c).wait_send()
-
-        @pl.when(me_col > 0)
-        def _():
-            to_left(c).wait_send()
-
-        return carry
-
-    lax.fori_loop(0, chunks, drain, 0)
-
-    @pl.when(me_row < n_row - 1)
-    def _():
-        to_down().wait_send()
-
-    @pl.when(me_row > 0)
-    def _():
-        to_up().wait_send()
-
-    out.wait()
-
-
-def side(me_col, me_ch, d, n_col, n_ch):
-    place = lax.rem(me_col * n_ch + me_ch + d, n_col * n_ch)
-    return {"col": place // n_ch, "ch": lax.rem(place, n_ch)}
-
-
-def smooth_kernel(field_ref, out_hbm, weight, first, second, done, out_sem):
-    rank, rows, cols = out_hbm.shape
-    wide = field_ref.shape[2]
-    groups = rank // SUB
-
-    def coefficients(e, carry):
-        center = field_ref[e, pl.ds(rank, SUB), :]
+    def coefficients(e):
+        center = field[e, pl.ds(rank, SUB), :]
         around = (
-            field_ref[e - 1, pl.ds(rank, SUB), :],
-            field_ref[e + 1, pl.ds(rank, SUB), :],
+            field[e - 1, pl.ds(rank, SUB), :],
+            field[e + 1, pl.ds(rank, SUB), :],
             pltpu.roll(center, 1, 1),
             pltpu.roll(center, wide - 1, 1),
         )
@@ -363,37 +314,130 @@
         weight[e, 0] = scale
         for j in range(4):
             weight[e, j + 1] = parts[j] * scale
-        return carry
-
-    lax.fori_loop(1, rows + 2 * SMOOTH - 1, coefficients, 0)
 
     def smooth(source, e):
-        here = source[e, pl.ds(0, rank), :].reshape(groups, SUB, wide)
-        up = source[e - 1, pl.ds(0, rank), :].reshape(groups, SUB, wide)
-        down = source[e + 1, pl.ds(0, rank), :].reshape(groups, SUB, wide)
+        here, up, down = (
+            source[at, pl.ds(0, rank), :].reshape(rank // SUB, SUB, wide)
+            for at in (e, e - 1, e + 1)
+        )
         total = weight[e, 0] * here + weight[e, 1] * up + weight[e, 2] * down
         total = total + weight[e, 3] * pltpu.roll(here, 1, 2)
         total = total + weight[e, 4] * pltpu.roll(here, wide - 1, 2)
         return total.reshape(rank, wide)
 
+    def put(r):
+        return pltpu.make_async_copy(done.at[r], out_hbm.at[:, r, :], out_sem.at[r])
+
     def one(e, carry):
-        first[e] = smooth(field_ref, e)
+        coefficients(e)
+        first[e] = smooth(field, e)
         return carry
 
     def two(e, carry):
         second[e] = smooth(first, e)
         return carry
 
-    def put(r):
-        return pltpu.make_async_copy(done.at[r], out_hbm.at[:, r, :], out_sem.at[r])
-
-    lax.fori_loop(1, rows + 5, one, 0)
-    lax.fori_loop(2, rows + 4, two, 0)
-    for r in range(rows):
-        done[r] = smooth(second, r + SMOOTH)[:, :cols]
-        put(r).start()
-    for r in range(rows):
+    def three(e, carry):
+        done[e - SMOOTH] = smooth(second, e)[:, :cols]
+        put(e - SMOOTH).start()
+        return carry
+
+    def sweep(starts, counts):
+        for stage, start, count in zip((one, two, three), starts, counts):
+            lax.fori_loop(0, count, lambda k, v, f=stage, s=start: f(s + k, v), 0)
+
+    def sweep_chunk(c):
+        sweep((CHUNK * c + 2, CHUNK * c + 1, CHUNK * c), (CHUNK,) * 3)
+
+    for i in range(2 * EDGE):
+        raise_chunk(i, awaited=i >= EDGE)
+    for i in range(2 * EDGE):
+        widen_chunk(i)
+
+    @pl.when(me_row < n_row - 1)
+    def _():
+        to_down().start()
+
+    @pl.when(me_row > 0)
+    def _():
+        to_up().start()
+
+    for i in range(2 * EDGE, 2 * EDGE + LAG):
+        raise_chunk(i)
+        if i > 2 * EDGE:
+            widen_chunk(i - 1)
+
+    @pl.when(me_row > 0)
+    def _():
+        to_down().wait_recv()
+
+    @pl.when(me_row < n_row - 1)
+    def _():
+        to_up().wait_recv()
+
+    tip = CHUNK * EDGE
+    sweep((1, 2, 3), (tip + 1, tip - 1, tip - 3))
+    for c in range(EDGE, EDGE + LAG - 1):
+        sweep_chunk(c)
+
+    def step(i, carry):
+        raise_chunk(i)
+        widen_chunk(i - 1)
+        sweep_chunk(i - 1 - EDGE)
+        return carry
+
+    lax.fori_loop(2 * EDGE + LAG, chunks, step, 0)
+    widen_chunk(chunks - 1)
+    sweep_chunk(chunks - 1 - EDGE)
+    sweep((early + 2, early + 1, early), (tip + 3,) * 3)
+
+    for d in range(1, n_col):
+        to_col(d).wait_send()
+    for d in range(1, n_row):
+        to_row(d).wait_send()
+    for d in range(1, n_col * n_ch):
+        to_side(d).wait_send()
+
+    def drain(c, carry):
+        @pl.when(me_col < n_col - 1)
+        def _():
+            to_right(c).wait_send()
+
+        @pl.when(me_col > 0)
+        def _():
+            to_left(c).wait_send()
+
+        return carry
+
+    lax.fori_loop(0, chunks, drain, 0)
+
+    def drain_part(i, carry):
+        for d in range(1, n_ch):
+            to_ch(d, chunk_of(i)).wait_send()
+        return carry
+
+    lax.fori_loop(EDGE, chunks, drain_part, 0)
+    for d in range(1, n_ch):
+        to_early(d).wait_send()
+
+    @pl.when(me_row < n_row - 1)
+    def _():
+        to_down().wait_send()
+
+    @pl.when(me_row > 0)
+    def _():
+        to_up().wait_send()
+
+    def drain_out(r, carry):
         put(r).wait()
+        return carry
+
+    lax.fori_loop(0, rows, drain_out, 0)
+
+
+def side(me_col, me_ch, d, n_col, n_ch):
+    place = lax.rem(me_col * n_ch + me_ch + d, n_col * n_ch)
+    return {"col": place // n_ch, "ch": lax.rem(place, n_ch)}
 
 
 def shards(sizes, spectra, pixel_factor, channel_factor, labels):
@@ -408,16 +452,17 @@
     vmem = pl.BlockSpec(memory_space=pltpu.VMEM)
     anywhere = pl.BlockSpec(memory_space=pl.ANY)
     dma = pltpu.SemaphoreType.DMA
-    field, new_channel = pl.pallas_call(
+    return pl.pallas_call(
         functools.partial(factor_kernel, sizes),
         out_shape=(
-            jax.ShapeDtypeStruct((tall, rank + SUB, wide), f32),
+            jax.ShapeDtypeStruct(pixel_factor.shape, f32),
             jax.ShapeDtypeStruct(channel_factor.shape, f32),
         ),
         in_specs=[anywhere, anywhere, vmem, vmem],
         out_specs=(anywhere, vmem),
         scratch_shapes=[
             pltpu.VMEM((rows, rank + chans, cols), f32),
+            pltpu.VMEM((n_ch - 1, EDGE * CHUNK, chans, cols), f32),
             pltpu.VMEM((n_col, share, rank + chans), f32),
             pltpu.VMEM((n_col - 1, share, rank + chans), f32),
             pltpu.VMEM((n_row, share, rank + chans), f32),
@@ -426,36 +471,25 @@
             pltpu.VMEM((tall, rank + SUB, wide), f32),
             pltpu.VMEM((rows, rank + SUB, LANES), f32),
             pltpu.VMEM((rows, rank + SUB, LANES), f32),
+            pltpu.VMEM((tall, 5, SUB, wide), f32),
+            pltpu.VMEM((tall, rank, wide), f32),
+            pltpu.VMEM((tall, rank, wide), f32),
+            pltpu.VMEM((rows, rank, cols), f32),
             dma((2, rows)),
+            dma((n_ch - 1,)), dma((n_ch - 1,)),
             dma((n_col - 1,)), dma((n_col - 1,)),
             dma((n_row - 1,)), dma((n_row - 1,)),
             dma((n_col * n_ch - 1,)), dma((n_col * n_ch - 1,)),
             dma((n_ch - 1, chunks)), dma((n_ch - 1, chunks)),
             dma((2, chunks)), dma((2, chunks)),
             dma((2,)), dma((2,)),
-            dma,
+            dma((rows,)),
         ],
         compiler_params=pltpu.CompilerParams(
             collective_id=0, has_side_effects=True, vmem_limit_bytes=60 * 1024 * 1024
         ),
         name="factor",
     )(spectra, pixel_factor, channel_factor, labels)
-    smoothed = pl.pallas_call(
-        smooth_kernel,
-        out_shape=jax.ShapeDtypeStruct(pixel_factor.shape, f32),
-        in_specs=[vmem],
-        out_specs=anywhere,
-        scratch_shapes=[
-            pltpu.VMEM((tall, 5, SUB, wide), f32),
-            pltpu.VMEM((tall, rank, wide), f32),
-            pltpu.VMEM((tall, rank, wide), f32),
-            pltpu.VMEM((rows, rank, cols), f32),
-            dma((rows,)),
-        ],
-        compiler_params=pltpu.CompilerParams(vmem_limit_bytes=48 * 1024 * 1024),
-        name="smooth",
-    )(field)
-    return smoothed, new_channel
 
 
 def solution(mesh):

time: 95.9 us -> 81.9 us (0.85)
  Pallas kernels: 92.2 us -> 77.2 us
  local copies, waits for them, and re-layouts: 2.82 us -> 3.82 us
    pallas_call x1 -> x0, Pallas kernels: 16.5 us -> none  [shards(): pl.pallas_call(smooth_kernel, out_shape=jax.ShapeDtypeStruct(pixel_factor...]
    pallas_call x1, Pallas kernels: 75.7 us -> 77.2 us  [shards(): pl.pallas_call(functools.partial(factor_kernel, sizes), out_shape=(jax.Sh...]
    unnamed x5 -> x4, local copies, waits for them, and re-layouts: 2.82 us -> 3.82 us
where the time goes in v2:
time: 81.9 us; the launch traced here: 81.7 us
  Pallas kernels  77.2 us (94%)
  local copies, waits for them, and re-layouts  3.82 us (5%)
    pallas_call x1, Pallas kernels, shards(): pl.pallas_call(functools.partial(factor_kernel, sizes), out_shape=(jax.Sh...  77.2 us
    unnamed x4, local copies, waits for them, and re-layouts  3.82 us

profile of v2, /device:TPU:1, one launch (start us, length us, event | category | flops | bytes accessed | tf_op | source)
XLA Modules:
  0.0 81.7 jit_solution(17195597788855589544)
XLA Ops:
  0.6 77.2 %factor.1 = (f32[64,32,256]{2,1,0:T(8,128)}, f32[64,192]{1,0:T(8,128)}) custom-call(f32[192,32,256]{2,1,0:T(8,128)} %x_hbm.1, f32[64,32,256]{2,1,0:T(8,128)} %w_hbm.1, f32[64,192]{1,0:T(8,128)} %cf_ref.1, s32[32,256]{1,0:T(8,128)} %lab_ref.1), custom_call_target="tpu_custom_call" | custom-call | tf_op jit(solution)/shard_map/factor/pallas_call | solution.py:455
  77.8 0.0 copy-start
  77.8 3.2 %copy.8 = f32[64,32,256]{2,1,0:T(8,128)} copy(f32[64,32,256]{2,1,0:T(8,128)} %get-tuple-element.4) | data formatting | bytes 4194304
  81.0 0.0 copy-done
  81.0 0.6 copy.9
Async XLA Ops:
  77.8 3.2 %copy-start = (f32[64,192]{1,0:T(8,128)S(1)}, f32[64,192]{1,0:T(8,128)}, u32[]{:S(2)}) copy-start(f32[64,192]{1,0:T(8,128)} %get-tuple-element.5) | copy-start | bytes 147460

commit v3 on v2

--- a/solution.py
+++ b/solution.py
@@ -42,7 +42,7 @@
 
 def factor_kernel(
     sizes, x_hbm, w_hbm, cf_ref, lab_ref, out_hbm, nc_out,
-    xw, other, gram, gram_in, gram_row, nc, part, field, left, right, weight, first, second, done,
+    xs, ws, other, gram, gram_in, gram_row, nc, part, field, left, right, weight, first, second, done,
     load_sem, e_send, e_recv, g_send, g_recv, z_send, z_recv, n_send, n_recv,
     t_send, t_recv, c_send, c_recv, r_send, r_recv, out_sem,
 ):
@@ -55,15 +55,32 @@
     wide = cols + LANES
     me_row, me_col, me_ch = (lax.axis_index(a) for a in ("row", "col", "ch"))
 
-    def load(r):
-        return (
-            pltpu.make_async_copy(w_hbm.at[:, r, :], xw.at[r, pl.ds(0, rank), :], load_sem.at[0, r]),
-            pltpu.make_async_copy(x_hbm.at[:, r, :], xw.at[r, pl.ds(rank, chans), :], load_sem.at[1, r]),
-        )
-
-    order = tuple(range(early, rows)) + tuple(range(early))
-    for r in order:
-        for copy in load(r):
+    halves = cols // LANES
+    groups = rows // SUB
+
+    def load(g):
+        for h in range(halves):
+            for j, (source, target) in enumerate(((w_hbm, ws), (x_hbm, xs))):
+                at = (slice(None), pl.ds(g * SUB, SUB))
+                yield pltpu.make_async_copy(
+                    source.at[at + (pl.ds(h * LANES, LANES),)],
+                    target.at[(h,) + at + (slice(None),)],
+                    load_sem.at[j, h, g],
+                )
+
+    def image_row(buffer, r):
+        _, depth, tall, _ = buffer.shape
+        return jnp.concatenate(
+            [
+                buffer.at[h].reshape(depth * tall, LANES)[pl.ds(r, depth, stride=tall), :]
+                for h in range(halves)
+            ],
+            axis=1,
+        )
+
+    order = tuple(range(groups - 1, -1, -1))
+    for g in order:
+        for copy in load(g):
             copy.start()
 
     barrier = pltpu.get_barrier_semaphore()
@@ -100,24 +117,24 @@
 
     def to_early(d):
         return pltpu.make_async_remote_copy(
-            xw.at[pl.ds(early, rows - early), pl.ds(rank, chans), :], other.at[d - 1],
+            xs.at[:, :, pl.ds(early, rows - early), :],
+            other.at[d - 1, :, :, pl.ds(early - rows + SUB, rows - early), :],
             e_send.at[d - 1], e_recv.at[d - 1],
             device_id={"ch": lax.rem(me_ch + d, n_ch)}, device_id_type=MESH,
         )
 
-    for r in order[: rows - early]:
-        for copy in load(r):
+    for i, g in enumerate(order):
+        for copy in load(g):
             copy.wait()
-    pl.semaphore_wait(barrier, n_row - 1 + n_col * n_ch - 1)
-    for d in range(1, n_ch):
-        to_early(d).start()
-    for i, r in enumerate(order):
-        if i >= rows - early:
-            for copy in load(r):
-                copy.wait()
-        high, low = split(xw[r])
-        total = dot3((high[:rank], low[:rank]), (high, low), NT)
-        gram[...] += total.reshape(gram.shape)
+        if i == 0:
+            pl.semaphore_wait(barrier, n_row - 1 + n_col * n_ch - 1)
+            for d in range(1, n_ch):
+                to_early(d).start()
+        for r in range(g * SUB, g * SUB + SUB):
+            both = jnp.concatenate([image_row(ws, r), image_row(xs, r)], axis=0)
+            high, low = split(both)
+            total = dot3((high[:rank], low[:rank]), (high, low), NT)
+            gram[...] += total.reshape(gram.shape)
 
     def to_col(d):
         peer = lax.rem(me_col + d, n_col)
@@ -208,7 +225,7 @@
         c = chunk_of(i)
         for k in range(CHUNK):
             r = c * CHUNK + k
-            part[me_ch, r] = dot3(mine, split(xw[r, pl.ds(rank, chans), :]), NN)
+            part[me_ch, r] = dot3(mine, split(image_row(xs, r)), NN)
         for d in range(1, n_ch):
             to_ch(d, c).start()
         return carry
@@ -216,13 +233,13 @@
     lax.fori_loop(EDGE, chunks, send_part, 0)
 
     for r in range(early, rows):
-        part[me_ch, r] = dot3(mine, split(xw[r, pl.ds(rank, chans), :]), NN)
+        part[me_ch, r] = dot3(mine, split(image_row(xs, r)), NN)
     for d in range(1, n_ch):
         peer = lax.rem(me_ch + n_ch - d, n_ch)
         theirs = split(nc[peer].reshape(rank, chans))
         to_early(d).wait_recv()
         for r in range(early, rows):
-            part[peer, r] = dot3(theirs, split(other[d - 1, r - early]), NN)
+            part[peer, r] = dot3(theirs, split(image_row(other.at[d - 1], r - rows + SUB)), NN)
 
     cg = jnp.zeros((rank, rank), jnp.float32)
     for h in range(n_ch):
@@ -254,7 +271,7 @@
                 from_ch(d, c).wait_recv()
         for k in range(CHUNK):
             r = c * CHUNK + k
-            w = xw[r, pl.ds(0, rank), :]
+            w = image_row(ws, r)
             top = part[0, r]
             for h in range(1, n_ch):
                 top = top + part[h, r]
@@ -461,8 +478,9 @@
         in_specs=[anywhere, anywhere, vmem, vmem],
         out_specs=(anywhere, vmem),
         scratch_shapes=[
-            pltpu.VMEM((rows, rank + chans, cols), f32),
-            pltpu.VMEM((n_ch - 1, EDGE * CHUNK, chans, cols), f32),
+            pltpu.VMEM((cols // LANES, chans, rows, LANES), f32),
+            pltpu.VMEM((cols // LANES, rank, rows, LANES), f32),
+            pltpu.VMEM((n_ch - 1, cols // LANES, chans, SUB, LANES), f32),
             pltpu.VMEM((n_col, share, rank + chans), f32),
             pltpu.VMEM((n_col - 1, share, rank + chans), f32),
             pltpu.VMEM((n_row, share, rank + chans), f32),
@@ -475,7 +493,7 @@
             pltpu.VMEM((tall, rank, wide), f32),
             pltpu.VMEM((tall, rank, wide), f32),
             pltpu.VMEM((rows, rank, cols), f32),
-            dma((2, rows)),
+            dma((2, cols // LANES, rows // SUB)),
             dma((n_ch - 1,)), dma((n_ch - 1,)),
             dma((n_col - 1,)), dma((n_col - 1,)),
             dma((n_row - 1,)), dma((n_row - 1,)),

time: 81.9 us -> 81.9 us (level)
  no operation moved by 1% of the time
where the time goes in v3:
time: 81.9 us; the launch traced here: 81.7 us
  Pallas kernels  77.2 us (94%)
  local copies, waits for them, and re-layouts  3.82 us (5%)
    pallas_call x1, Pallas kernels, shards(): pl.pallas_call(functools.partial(factor_kernel, sizes), out_shape=(jax.Sh...  77.2 us
    unnamed x4, local copies, waits for them, and re-layouts  3.82 us

profile of v3, /device:TPU:1, one launch (start us, length us, event | category | flops | bytes accessed | tf_op | source)
XLA Modules:
  0.0 81.7 jit_solution(14788095919101881360)
XLA Ops:
  0.6 77.2 %factor.1 = (f32[64,32,256]{2,1,0:T(8,128)}, f32[64,192]{1,0:T(8,128)}) custom-call(f32[192,32,256]{2,1,0:T(8,128)} %x_hbm.1, f32[64,32,256]{2,1,0:T(8,128)} %w_hbm.1, f32[64,192]{1,0:T(8,128)} %cf_ref.1, s32[32,256]{1,0:T(8,128)} %lab_ref.1), custom_call_target="tpu_custom_call" | custom-call | tf_op jit(solution)/shard_map/factor/pallas_call | solution.py:472
  77.8 0.0 copy-start
  77.8 3.2 %copy.8 = f32[64,32,256]{2,1,0:T(8,128)} copy(f32[64,32,256]{2,1,0:T(8,128)} %get-tuple-element.4) | data formatting | bytes 4194304
  81.0 0.0 copy-done
  81.0 0.6 copy.9
Async XLA Ops:
  77.8 3.2 %copy-start = (f32[64,192]{1,0:T(8,128)S(1)}, f32[64,192]{1,0:T(8,128)}, u32[]{:S(2)}) copy-start(f32[64,192]{1,0:T(8,128)} %get-tuple-element.5) | copy-start | bytes 147460

commit v4 on v3

--- a/solution.py
+++ b/solution.py
@@ -13,7 +13,7 @@
 SUB = 8
 CHUNK = 2
 EDGE = -(-SMOOTH // CHUNK)
-LAG = 3
+LAG = 4
 
 epsilon = 1e-09
 
@@ -381,8 +381,8 @@
 
     for i in range(2 * EDGE, 2 * EDGE + LAG):
         raise_chunk(i)
-        if i > 2 * EDGE:
-            widen_chunk(i - 1)
+        if i > 2 * EDGE + 1:
+            widen_chunk(i - 2)
 
     @pl.when(me_row > 0)
     def _():
@@ -394,18 +394,19 @@
 
     tip = CHUNK * EDGE
     sweep((1, 2, 3), (tip + 1, tip - 1, tip - 3))
-    for c in range(EDGE, EDGE + LAG - 1):
+    for c in range(EDGE, EDGE + LAG - 2):
         sweep_chunk(c)
 
     def step(i, carry):
+        widen_chunk(i - 2)
+        sweep_chunk(i - 2 - EDGE)
         raise_chunk(i)
-        widen_chunk(i - 1)
-        sweep_chunk(i - 1 - EDGE)
         return carry
 
     lax.fori_loop(2 * EDGE + LAG, chunks, step, 0)
-    widen_chunk(chunks - 1)
-    sweep_chunk(chunks - 1 - EDGE)
+    for i in (chunks - 2, chunks - 1):
+        widen_chunk(i)
+        sweep_chunk(i - EDGE)
     sweep((early + 2, early + 1, early), (tip + 3,) * 3)
 
     for d in range(1, n_col):

time: 81.9 us -> 81.9 us (level)
  no operation moved by 1% of the time
where the time goes in v4:
time: 81.9 us; the launch traced here: 81.7 us
  Pallas kernels  77.2 us (94%)
  local copies, waits for them, and re-layouts  3.82 us (5%)
    pallas_call x1, Pallas kernels, shards(): pl.pallas_call(functools.partial(factor_kernel, sizes), out_shape=(jax.Sh...  77.2 us
    unnamed x4, local copies, waits for them, and re-layouts  3.82 us

profile of v4, /device:TPU:1, one launch (start us, length us, event | category | flops | bytes accessed | tf_op | source)
XLA Modules:
  0.0 81.7 jit_solution(16996479479510228968)
XLA Ops:
  0.6 77.2 %factor.1 = (f32[64,32,256]{2,1,0:T(8,128)}, f32[64,192]{1,0:T(8,128)}) custom-call(f32[192,32,256]{2,1,0:T(8,128)} %x_hbm.1, f32[64,32,256]{2,1,0:T(8,128)} %w_hbm.1, f32[64,192]{1,0:T(8,128)} %cf_ref.1, s32[32,256]{1,0:T(8,128)} %lab_ref.1), custom_call_target="tpu_custom_call" | custom-call | tf_op jit(solution)/shard_map/factor/pallas_call | solution.py:473
  77.8 0.0 copy-start
  77.8 3.2 %copy.8 = f32[64,32,256]{2,1,0:T(8,128)} copy(f32[64,32,256]{2,1,0:T(8,128)} %get-tuple-element.4) | data formatting | bytes 4194304
  81.0 0.0 copy-done
  81.0 0.6 copy.9
Async XLA Ops:
  77.8 3.2 %copy-start = (f32[64,192]{1,0:T(8,128)S(1)}, f32[64,192]{1,0:T(8,128)}, u32[]{:S(2)}) copy-start(f32[64,192]{1,0:T(8,128)} %get-tuple-element.5) | copy-start | bytes 147460
